TPU v7x, 32 devices: a whole 2x2x4 slice. The times are simulated.
32 devices in a mesh: dp: 8 (over y, x, core), mp: 4 (over z).
Axes of the slice: x: 2, y: 2, z: 4, core: 2. Of those that a mesh axis runs over, the one named last changes fastest.
Arguments:
- frames: bfloat16 [8192, 1024], P(('dp', 'mp')), may hold values from -6 to 6
- lengths: int32 [8, 6], P('dp'), may hold values from 1 to 682, 896 in all within a row
- w_qkv: bfloat16 [3, 1024, 1024], P(None, None, 'mp'), may hold values from -0.1875 to 0.1875
- w_attn_out: bfloat16 [1024, 1024], P('mp'), may hold values from -0.5 to 0.5
- w_in: bfloat16 [1024, 4096], P(None, 'mp'), may hold values from -0.1875 to 0.1875
- w_out: bfloat16 [4096, 1024], P('mp'), may hold values from -0.09375 to 0.09375
- gain_attn: float32 [1024], replicated, may hold values from 0.5 to 1.5
- gain_mlp: float32 [1024], replicated, may hold values from 0.5 to 1.5
- cotangent: bfloat16 [8192, 1024], P(('dp', 'mp')), may hold values from -6 to 6
Outputs:
- output: bfloat16 [8192, 1024], P(('dp', 'mp'))
- grad_frames: float32 [8192, 1024], P(('dp', 'mp'))
- grad_w_qkv: float32 [3, 1024, 1024], P(None, None, 'mp')
- grad_w_attn_out: float32 [1024, 1024], P('mp')
- grad_w_in: float32 [1024, 4096], P(None, 'mp')
- grad_w_out: float32 [4096, 1024], P('mp')
- grad_gain_attn: float32 [1024], replicated
- grad_gain_mlp: float32 [1024], replicated
Inputs may be any that keep to these rules, and one draw needn't show every extreme that they name: `lengths`: each row holds the frame counts of the 6 items of one batch; they sum to 896 and the largest is exactly 682; the remaining frames of the batch are padding.
All inputs are finite; a program needn't handle non-finite values.
Results may differ from a plain program's by a relative error of at most 0.012.
Values may be sent and summed in bfloat16 or wider, within the bound.
A program may use at most 128 MiB of HBM per device.

v0:
```python
import jax
import jax.numpy as jnp
from jax import lax
from jax.sharding import PartitionSpec as P

HEAD = 64
BLOCK = 512
EPSILON = 1e-06
NEGATIVE = -1e30


def rms_scale(values, scaling_gain):
    return (
        values
        * lax.rsqrt(jnp.mean(values * values, axis=-1, keepdims=True) + EPSILON)
        * scaling_gain
    )


def gelu_tanh(values):
    return jax.nn.gelu(values, approximate=True)


def item_ids(length_row, frame_count):
    item_ends = jnp.cumsum(length_row)
    positions = jnp.arange(frame_count, dtype=jnp.int32)
    before = jnp.sum((positions[:, None] >= item_ends[None, :]).astype(jnp.int32), axis=1)
    return jnp.where(positions < item_ends[-1], before, before + positions + 1)


def block_scores(queries, positions, idents, keys_all, idents_all, scaling):
    scores = (
        jnp.einsum("bhd,khd->hbk", queries, keys_all, preferred_element_type=jnp.float32) * scaling
    )
    frame_count = keys_all.shape[0]
    visible = (idents[:, None] == idents_all[None, :]) & (
        jnp.arange(frame_count, dtype=jnp.int32)[None, :] <= positions[:, None]
    )
    return (scores, visible[None])


def per_device(frames, lengths, w_qkv, w_attn_out, w_in, w_out, gain_attn, gain_mlp, cotangent):
    frame_count = frames.shape[0] * lax.axis_size("mp")
    heads_here = w_attn_out.shape[0] // HEAD
    scaling = HEAD ** (-0.5)
    idents = item_ids(lengths[0], frame_count)
    positions = jnp.arange(frame_count, dtype=jnp.int32)
    frames_wide = frames.astype(jnp.float32)
    normed = rms_scale(frames_wide, gain_attn).astype(jnp.bfloat16)
    normed_all = lax.all_gather(normed, "mp", axis=0, tiled=True)
    projected = jnp.einsum(
        "td,cde->cte", normed_all, w_qkv, preferred_element_type=jnp.float32
    ).astype(jnp.bfloat16)
    head_split = projected.reshape(3, frame_count, heads_here, HEAD)
    queries, keys_all, values_all = (head_split[0], head_split[1], head_split[2])
    blocks = frame_count // BLOCK
    outputs = []
    log_totals = []
    for number in range(blocks):
        window = slice(number * BLOCK, (number + 1) * BLOCK)
        scores, visible = block_scores(
            queries[window], positions[window], idents[window], keys_all, idents, scaling
        )
        masked = jnp.where(visible, scores, NEGATIVE)
        row_peak = jnp.max(masked, axis=-1, keepdims=True)
        weights = jnp.where(visible, jnp.exp(masked - row_peak), 0.0)
        row_total = jnp.sum(weights, axis=-1, keepdims=True)
        probabilities = weights / row_total
        outputs.append(
            jnp.einsum(
                "hbk,khd->bhd",
                probabilities.astype(jnp.bfloat16),
                values_all,
                preferred_element_type=jnp.float32,
            )
        )
        log_totals.append(row_peak + jnp.log(row_total))
    attended = (
        jnp.concatenate(outputs, axis=0)
        .reshape(frame_count, heads_here * HEAD)
        .astype(jnp.bfloat16)
    )
    attn_part = jnp.dot(attended, w_attn_out, preferred_element_type=jnp.float32)
    attn_own = lax.psum_scatter(attn_part, "mp", scatter_dimension=0, tiled=True)
    resid = frames_wide + attn_own
    normed_mlp = rms_scale(resid, gain_mlp).astype(jnp.bfloat16)
    normed_mlp_all = lax.all_gather(normed_mlp, "mp", axis=0, tiled=True)
    hidden = jnp.dot(normed_mlp_all, w_in, preferred_element_type=jnp.float32)
    active = gelu_tanh(hidden).astype(jnp.bfloat16)
    mlp_own = lax.psum_scatter(
        jnp.dot(active, w_out, preferred_element_type=jnp.float32).astype(jnp.bfloat16),
        "mp",
        scatter_dimension=0,
        tiled=True,
    ).astype(jnp.float32)
    output = (resid + mlp_own).astype(jnp.bfloat16)
    grad_top = cotangent.astype(jnp.float32)
    grad_all = lax.all_gather(cotangent, "mp", axis=0, tiled=True)
    grad_w_out = jnp.einsum("tf,td->fd", active, grad_all, preferred_element_type=jnp.float32)
    grad_active = jnp.einsum("td,fd->tf", grad_all, w_out, preferred_element_type=jnp.float32)
    grad_hidden = jax.vjp(gelu_tanh, hidden)[1](grad_active)[0].astype(jnp.bfloat16)
    grad_w_in = jnp.einsum(
        "td,tf->df", normed_mlp_all, grad_hidden, preferred_element_type=jnp.float32
    )
    grad_normed_mlp = lax.psum_scatter(
        jnp.einsum("tf,df->td", grad_hidden, w_in, preferred_element_type=jnp.float32),
        "mp",
        scatter_dimension=0,
        tiled=True,
    )
    resid_back, gain_mlp_part = jax.vjp(rms_scale, resid, gain_mlp)[1](grad_normed_mlp)
    grad_resid = grad_top + resid_back
    grad_resid_all = lax.all_gather(grad_resid.astype(jnp.bfloat16), "mp", axis=0, tiled=True)
    grad_w_attn_out = jnp.einsum(
        "te,td->ed", attended, grad_resid_all, preferred_element_type=jnp.float32
    )
    grad_attended = (
        jnp.einsum("td,ed->te", grad_resid_all, w_attn_out, preferred_element_type=jnp.float32)
        .astype(jnp.bfloat16)
        .reshape(frame_count, heads_here, HEAD)
    )
    grad_keys = jnp.zeros((frame_count, heads_here, HEAD), jnp.float32)
    grad_values = jnp.zeros((frame_count, heads_here, HEAD), jnp.float32)
    grad_queries = []
    for number in range(blocks):
        window = slice(number * BLOCK, (number + 1) * BLOCK)
        scores, visible = block_scores(
            queries[window], positions[window], idents[window], keys_all, idents, scaling
        )
        probabilities = jnp.where(
            visible, jnp.exp(jnp.where(visible, scores, NEGATIVE) - log_totals[number]), 0.0
        )
        grad_rows = grad_attended[window]
        grad_probs = jnp.einsum(
            "bhd,khd->hbk", grad_rows, values_all, preferred_element_type=jnp.float32
        )
        grad_values = grad_values + jnp.einsum(
            "hbk,bhd->khd",
            probabilities.astype(jnp.bfloat16),
            grad_rows,
            preferred_element_type=jnp.float32,
        )
        inner_sum = jnp.sum(probabilities * grad_probs, axis=-1, keepdims=True)
        grad_scores = (probabilities * (grad_probs - inner_sum)).astype(jnp.bfloat16)
        grad_queries.append(
            jnp.einsum("hbk,khd->bhd", grad_scores, keys_all, preferred_element_type=jnp.float32)
            * scaling
        )
        grad_keys = (
            grad_keys
            + jnp.einsum(
                "hbk,bhd->khd", grad_scores, queries[window], preferred_element_type=jnp.float32
            )
            * scaling
        )
    grad_projected = jnp.stack(
        [
            jnp.concatenate(grad_queries, axis=0).reshape(frame_count, heads_here * HEAD),
            grad_keys.reshape(frame_count, heads_here * HEAD),
            grad_values.reshape(frame_count, heads_here * HEAD),
        ]
    ).astype(jnp.bfloat16)
    grad_w_qkv = jnp.einsum(
        "td,cte->cde", normed_all, grad_projected, preferred_element_type=jnp.float32
    )
    grad_normed = lax.psum_scatter(
        jnp.einsum("cte,cde->td", grad_projected, w_qkv, preferred_element_type=jnp.float32),
        "mp",
        scatter_dimension=0,
        tiled=True,
    )
    frames_back, gain_attn_part = jax.vjp(rms_scale, frames_wide, gain_attn)[1](grad_normed)
    grad_frames = grad_resid + frames_back
    grad_gain_attn, grad_gain_mlp = lax.psum((gain_attn_part, gain_mlp_part), ("dp", "mp"))
    grad_w_qkv, grad_w_attn_out, grad_w_in, grad_w_out = lax.psum(
        (grad_w_qkv, grad_w_attn_out, grad_w_in, grad_w_out), "dp"
    )
    return (
        output,
        grad_frames,
        grad_w_qkv,
        grad_w_attn_out,
        grad_w_in,
        grad_w_out,
        grad_gain_attn,
        grad_gain_mlp,
    )


def solution(mesh):
    in_specs = (
        P(("dp", "mp"), None),
        P("dp", None),
        P(None, None, "mp"),
        P("mp", None),
        P(None, "mp"),
        P("mp", None),
        P(),
        P(),
        P(("dp", "mp"), None),
    )
    out_specs = (
        P(("dp", "mp"), None),
        P(("dp", "mp"), None),
        P(None, None, "mp"),
        P("mp", None),
        P(None, "mp"),
        P("mp", None),
        P(),
        P(),
    )
    return jax.shard_map(
        per_device, mesh=mesh, in_specs=in_specs, out_specs=out_specs, check_vma=False
    )
```

profile of v0, /device:TPU:0, one launch (start us, length us, event | category | flops | bytes accessed | tf_op | source)
XLA Modules:
  0.0 765.5 jit_solution(12484631126287785952)
XLA Ops:
  14.7 44.8 %all-gather.5.cloned.1.call-done = bf16[1024,1024]{1,0:T(8,128)(2,1)} async-done(((bf16[256,1024]{1,0:T(8,128)(2,1)}), bf16[1024,1024]{1,0:T(8,128)(2,1)}) %all-gather.5.cloned.1.call-update) | async-done | bytes 2097168 | tf_op jit(solution)/shard_map/all_gather | solution.py:50
  59.5 3.9 fusion.29
  84.2 74.4 %reduce-scatter.5.cloned.1.call-done = f32[256,1024]{1,0:T(8,128)} async-done(((f32[1024,1024]{1,0:T(8,128)}), f32[256,1024]{1,0:T(8,128)}) %reduce-scatter.5.cloned.1.call-update) | async-done | bytes 1048592 | tf_op jit(solution)/shard_map/reduce_scatter | solution.py:84
  161.2 45.5 %all-gather.9.cloned.1.call-done = bf16[1024,1024]{1,0:T(8,128)(2,1)} async-done(((bf16[256,1024]{1,0:T(8,128)(2,1)}), bf16[1024,1024]{1,0:T(8,128)(2,1)}) %all-gather.9.cloned.1.call-update) | async-done | bytes 2097168 | tf_op jit(solution)/shard_map/all_gather | solution.py:98
  206.8 6.6 fusion.79
  213.4 40.2 %all-gather.7.cloned.1.call-done = bf16[1024,1024]{1,0:T(8,128)(2,1)} async-done(((bf16[256,1024]{1,0:T(8,128)(2,1)}), bf16[1024,1024]{1,0:T(8,128)(2,1)}) %all-gather.7.cloned.1.call-update) | async-done | bytes 2097168 | tf_op jit(solution)/shard_map/all_gather | solution.py:87
  253.5 8.2 %fusion.10 = (bf16[1024,1024]{1,0:T(8,128)(2,1)S(1)}, f32[1024,1024]{1,0:T(8,128)}) fusion(f32[1024,1024]{1,0:T(8,128)} %fusion.79, bf16[1024,1024]{1,0:T(8,128)(2,1)} %all-gather.7.cloned.1.call-done, bf16[1024,1024]{1,0:T(8,128)(2,1)S(1)} %copy-done), kind=kOutput, calls=%fused_computation.24 | convolution fusion | flops 2168455168 | bytes 14680064 | tf_op jit(solution)/shard_map/dot_general | solution.py:88
  263.1 4.4 fusion.80
  267.6 75.6 %reduce-scatter.9.cloned.1.call-done = f32[256,1024]{1,0:T(8,128)} async-done(((f32[1024,1024]{1,0:T(8,128)}), f32[256,1024]{1,0:T(8,128)}) %reduce-scatter.9.cloned.1.call-update) | async-done | bytes 1048592 | tf_op jit(solution)/shard_map/reduce_scatter | solution.py:105
  347.3 6.7 fusion.83
  354.0 4.8 fusion.73
  358.8 34.8 %all-gather.11.cloned.1.call-done = bf16[1024,1024]{1,0:T(8,128)(2,1)} async-done(((bf16[256,1024]{1,0:T(8,128)(2,1)}), bf16[1024,1024]{1,0:T(8,128)(2,1)}) %all-gather.11.cloned.1.call-update) | async-done | bytes 2097168 | tf_op jit(solution)/shard_map/all_gather | solution.py:113
  396.2 5.2 fusion.11
  401.5 5.7 multiply_reduce_fusion
  407.2 5.8 multiply_reduce_fusion.1
  413.0 10.5 %multiply_convert_fusion = (bf16[4,512,1024]{2,1,0:T(8,128)(2,1)}, bf16[4,512,1024]{2,1,0:T(8,128)(2,1)S(1)}) fusion(f32[4,512,1024]{2,1,0:T(8,128)} %get-tuple-element.57, f32[4,512]{1,0:T(4,128)S(1)} %get-tuple-element.56, f32[4,512]{1,0:T(4,128)S(1)} %log_add_fusion, f32[4,512,1024]{2,1,0:T(8,128)S(1)} %bitcast.83, pred[512,1024]{1,0:T(8,128)(4,1)S(1)} %copy-done.12, ...), kind=kLoop, calls=%fused_computation | loop fusion | flops 29360128 | bytes 43024384 | tf_op jit(solution)/shard_map/convert_element_type | solution.py:144
  431.8 4.4 fusion.48
  443.6 5.3 fusion.23
  449.9 5.2 convolution_bitcast_fusion
  456.8 6.3 convolution_convert_fusion
  463.1 158.1 %all-reduce.4.cloned.1.call-done = (f32[3,1024,256]{1,2,0:T(8,128)}, f32[256,1024]{1,0:T(8,128)}, f32[1024,1024]{1,0:T(8,128)}, f32[1024,1024]{1,0:T(8,128)}) async-done(((f32[3,1024,256]{1,2,0:T(8,128)}, f32[256,1024]{1,0:T(8,128)}, f32[1024,1024]{1,0:T(8,128)}, f32[1024,1024]{1,0:T(8,128)}), (f32[3,1024,256]{1,2,0:T(8,128)}, f32[256,1024]{1,0:T(8,128)}, f32[1024,1024]{1,0:T(8,128)}, ...) | async-done | bytes 12582928 | tf_op jit(solution)/shard_map/psum | solution.py:175
  621.2 3.5 copy.28
  624.7 76.3 %reduce-scatter.11.cloned.1.call-done = f32[256,1024]{1,0:T(8,128)} async-done(((f32[1024,1024]{1,0:T(8,128)}), f32[256,1024]{1,0:T(8,128)}) %reduce-scatter.11.cloned.1.call-update) | async-done | bytes 1048592 | tf_op jit(solution)/shard_map/reduce_scatter | solution.py:166
  702.6 43.7 %all-reduce = (f32[1024]{0:T(1024)}, f32[1024]{0:T(1024)}) all-reduce(f32[1024]{0:T(1024)S(1)} %get-tuple-element.26, f32[1024]{0:T(1024)S(1)} %get-tuple-element.24), channel_id=1, replica_groups=mesh['dp'=8,'mp'=4] {'dp','mp'}, use_global_device_ids=true, to_apply=%region_21.22 | all-reduce | flops 2048 | bytes 16384 | tf_op jit(solution)/shard_map/psum | solution.py:174
  (147 shorter events, 70.8 us)
Async XLA Ops:
  7.2 246.4 %copy-start = (bf16[1024,1024]{1,0:T(8,128)(2,1)S(1)}, bf16[1024,1024]{1,0:T(8,128)(2,1)}, u32[]{:S(2)}) copy-start(bf16[1024,1024]{1,0:T(8,128)(2,1)} %param.13) | copy-start | bytes 6291460
  7.2 52.3 %all-gather.5.cloned.1.call-start = ((), (), s32[]{:S(2)}) async-start(), calls=%async_computation.4 | async-start | bytes 2621440 | tf_op jit(solution)/shard_map/all_gather | solution.py:50
  10.7 148.0 %reduce-scatter.5.cloned.1.call-start = ((), (), s32[]{:S(2)}) async-start(), calls=%async_computation.5 | async-start | bytes 5242880 | tf_op jit(solution)/shard_map/reduce_scatter | solution.py:84
  14.7 61.7 %copy-start.9 = (pred[512,1024]{1,0:T(8,128)(4,1)}, pred[512,1024]{1,0:T(8,128)(4,1)S(1)}, u32[]{:S(2)}) copy-start(pred[512,1024]{1,0:T(8,128)(4,1)S(1)} %get-tuple-element.44) | copy-start | bytes 1572868
  63.4 8.4 %copy-start.19 = (bf16[1,512,256]{1,2,0:T(8,128)(2,1)}, bf16[1,512,256]{1,2,0:T(8,128)(2,1)S(1)}, u32[]{:S(2)}) copy-start(bf16[1,512,256]{1,2,0:T(8,128)(2,1)S(1)} %get-tuple-element.36) | copy-start | bytes 786436
  63.5 8.3 %copy-start.5 = (bf16[1,1024,256]{1,2,0:T(8,128)(2,1)}, bf16[1,1024,256]{1,2,0:T(8,128)(2,1)S(1)}, u32[]{:S(2)}) copy-start(bf16[1,1024,256]{1,2,0:T(8,128)(2,1)S(1)} %get-tuple-element.38) | copy-start | bytes 1572868
  63.5 12.9 %copy-start.27 = (bf16[1,1024,256]{1,2,0:T(8,128)(2,1)}, bf16[1,1024,256]{1,2,0:T(8,128)(2,1)S(1)}, u32[]{:S(2)}) copy-start(bf16[1,1024,256]{1,2,0:T(8,128)(2,1)S(1)} %get-tuple-element.39) | copy-start | bytes 1572868
  83.0 77.2 %copy-start.29 = (f32[1024]{0:T(1024)S(1)}, f32[1024]{0:T(1024)}, u32[]{:S(2)}) copy-start(f32[1024]{0:T(1024)} %param.16) | copy-start | bytes 12292
  83.0 123.8 %all-gather.9.cloned.1.call-start = ((), (), s32[]{:S(2)}) async-start(), calls=%async_computation.8 | async-start | bytes 2621440 | tf_op jit(solution)/shard_map/all_gather | solution.py:98
  83.7 169.8 %all-gather.7.cloned.1.call-start = ((), (), s32[]{:S(2)}) async-start(), calls=%async_computation.6 | async-start | bytes 2621440 | tf_op jit(solution)/shard_map/all_gather | solution.py:87
  161.2 182.0 %reduce-scatter.9.cloned.1.call-start = ((), (), s32[]{:S(2)}) async-start(), calls=%async_computation.9 | async-start | bytes 5242880 | tf_op jit(solution)/shard_map/reduce_scatter | solution.py:105
  267.5 77.1 %copy-start.15 = (bf16[256,1024]{1,0:T(8,128)(2,1)S(1)}, bf16[256,1024]{1,0:T(8,128)(2,1)}, u32[]{:S(2)}) copy-start(bf16[256,1024]{1,0:T(8,128)(2,1)} %param.17) | copy-start | bytes 1572868
  267.6 126.1 %all-gather.11.cloned.1.call-start = ((), (), s32[]{:S(2)}) async-start(), calls=%async_computation.10 | async-start | bytes 2621440 | tf_op jit(solution)/shard_map/all_gather | solution.py:113
  347.0 274.1 %all-reduce.4.cloned.1.call-start = ((), (), s32[]{:S(2)}) async-start(), calls=%async_computation.12 | async-start | bytes 25165824 | tf_op jit(solution)/shard_map/psum | solution.py:175
  354.0 39.6 %copy-start.23 = (bf16[256,1024]{1,0:T(8,128)(2,1)S(1)}, bf16[256,1024]{1,0:T(8,128)(2,1)}, u32[]{:S(2)}) copy-start(bf16[256,1024]{1,0:T(8,128)(2,1)} %param.12) | copy-start | bytes 1572868
  358.8 37.3 %copy-start.12 = (pred[512,1024]{1,0:T(8,128)(4,1)S(1)}, pred[512,1024]{1,0:T(8,128)(4,1)}, u32[]{:S(2)}) copy-start(pred[512,1024]{1,0:T(8,128)(4,1)} %get-tuple-element.45) | copy-start | bytes 1572868
  396.2 11.0 %slice-start = ((s8[8388608]{0:T(1024)(128)(4,1)}), s8[4194304]{0:T(1024)(128)(4,1)S(1)}, s32[]{:S(2)}) async-start(s8[8388608]{0:T(1024)(128)(4,1)} %bitcast.80), calls=%async_computation.13 | async-start | bytes 8388608
  413.0 10.5 %copy-start.6 = (bf16[1,1024,256]{1,2,0:T(8,128)(2,1)S(1)}, bf16[1,1024,256]{1,2,0:T(8,128)(2,1)}, u32[]{:S(2)}) copy-start(bf16[1,1024,256]{1,2,0:T(8,128)(2,1)} %copy-done.5) | copy-start | bytes 1572868
  448.9 252.1 %reduce-scatter.11.cloned.1.call-start = ((), (), s32[]{:S(2)}) async-start(), calls=%async_computation.11 | async-start | bytes 5242880 | tf_op jit(solution)/shard_map/reduce_scatter | solution.py:166
  455.2 293.6 %reduce-scatter.7.cloned.1.call-start = ((), (), s32[]{:S(2)}) async-start(), calls=%async_computation.7 | async-start | bytes 2621440 | tf_op jit(solution)/shard_map/reduce_scatter | solution.py:90
  463.0 238.0 %copy-start.7 = (bf16[256,1024]{1,0:T(8,128)(2,1)S(1)}, bf16[256,1024]{1,0:T(8,128)(2,1)}, u32[]{:S(2)}) copy-start(bf16[256,1024]{1,0:T(8,128)(2,1)} %param.9) | copy-start | bytes 1572868
  463.0 238.0 %copy-start.30 = (f32[1024]{0:T(1024)S(1)}, f32[1024]{0:T(1024)}, u32[]{:S(2)}) copy-start(f32[1024]{0:T(1024)} %param.15) | copy-start | bytes 12292
  463.0 285.7 %copy-start.8 = (f32[256,1024]{1,0:T(8,128)S(1)}, f32[256,1024]{1,0:T(8,128)}, u32[]{:S(2)}) copy-start(f32[256,1024]{1,0:T(8,128)} %reduce-scatter.9.cloned.1.call-done) | copy-start | bytes 3145732
  463.1 285.7 %copy-start.16 = (bf16[256,1024]{1,0:T(8,128)(2,1)S(1)}, bf16[256,1024]{1,0:T(8,128)(2,1)}, u32[]{:S(2)}) copy-start(bf16[256,1024]{1,0:T(8,128)(2,1)} %param.17) | copy-start | bytes 1572868
  (24 other events, 103.1 us)
Sparse Core Ops, SparseCore 0:
  10.8 48.6 all-gather.4
  83.1 75.4 reduce-scatter.4
  160.3 46.4 all-gather.8
  208.8 44.6 all-gather.6
  267.7 75.4 reduce-scatter.8
  347.2 46.4 all-gather.10
  449.0 172.0 all-reduce.3
  624.1 76.8 reduce-scatter.10
  703.3 45.3 reduce-scatter.6
where the time goes:
time: 774 us; the launch traced here: 766 us
  waiting for transfers between devices  553 us (71%)
  matrix products  98.3 us (13%)
  blocking collectives  43.7 us (6%)
  other arithmetic  35.4 us (5%)
  local copies, waits for them, and re-layouts  19.6 us (3%)
  between operations  14.7 us (2%)
    psum x1, waiting for transfers between devices, per_device(): lax.psum((grad_w_qkv, grad_w_attn_out, grad_w_in, grad_w_out), 'dp')  158 us
    reduce_scatter x1, waiting for transfers between devices, per_device(): lax.psum_scatter(jnp.einsum('cte,cde->td', grad_projected, w_qkv, preferr...  76.3 us
    reduce_scatter x1, waiting for transfers between devices, per_device(): lax.psum_scatter(jnp.einsum('tf,df->td', grad_hidden, w_in, preferred_ele...  75.6 us
    reduce_scatter x1, waiting for transfers between devices, per_device(): lax.psum_scatter(attn_part, 'mp', scatter_dimension=0, tiled=True)  74.4 us
    all_gather x1, waiting for transfers between devices, per_device(): grad_all = lax.all_gather(cotangent, 'mp', axis=0, tiled=True)  45.5 us
    all_gather x1, waiting for transfers between devices, per_device(): normed_all = lax.all_gather(normed, 'mp', axis=0, tiled=True)  44.8 us
    psum x1, blocking collectives, per_device(): lax.psum((gain_attn_part, gain_mlp_part), ('dp', 'mp'))  43.7 us
    all_gather x1, waiting for transfers between devices, per_device(): normed_mlp_all = lax.all_gather(normed_mlp, 'mp', axis=0, tiled=True)  40.2 us
  transfers between devices with their start and end apart: 9, of which 9 were waited for; matrix products, arithmetic and copies ran while one was open for 5% of the time, Pallas kernels for 0%

commit v1 on v0

--- a/solution.py
+++ b/solution.py
@@ -95,7 +95,12 @@
     ).astype(jnp.float32)
     output = (resid + mlp_own).astype(jnp.bfloat16)
     grad_top = cotangent.astype(jnp.float32)
-    grad_all = lax.all_gather(cotangent, "mp", axis=0, tiled=True)
+    ring = [cotangent]
+    for hop in range(3):
+        ring.append(lax.ppermute(ring[-1], "mp", [(dev, (dev + 1) % 4) for dev in range(4)]))
+    grad_all = jnp.roll(
+        jnp.concatenate(ring[::-1], axis=0), (lax.axis_index("mp") + 1) * ring[0].shape[0], axis=0
+    )
     grad_w_out = jnp.einsum("tf,td->fd", active, grad_all, preferred_element_type=jnp.float32)
     grad_active = jnp.einsum("td,fd->tf", grad_all, w_out, preferred_element_type=jnp.float32)
     grad_hidden = jax.vjp(gelu_tanh, hidden)[1](grad_active)[0].astype(jnp.bfloat16)

time: 774 us -> 772 us (level)
  waiting for transfers between devices: 553 us -> 516 us
  starting transfers between devices: 1.01 us -> 21.5 us
  local copies, waits for them, and re-layouts: 19.6 us -> 33.3 us
    ppermute x0 -> x3, waiting for transfers between devices: none -> 51 us  [per_device(): lax.ppermute(ring[-1], 'mp', [(dev, (dev + 1) % 4) for dev in range(4)])]
    all_gather x1 -> x0, waiting for transfers between devices: 45.5 us -> none  [per_device(): grad_all = lax.all_gather(cotangent, 'mp', axis=0, tiled=True)]
    all_gather x1, waiting for transfers between devices: 40.2 us -> 0.01 us  [per_device(): normed_mlp_all = lax.all_gather(normed_mlp, 'mp', axis=0, tiled=True)]
    ppermute x0 -> x3, starting transfers between devices: none -> 20.5 us  [per_device(): lax.ppermute(ring[-1], 'mp', [(dev, (dev + 1) % 4) for dev in range(4)])]
    unnamed x82 -> x97, local copies, waits for them, and re-layouts: 14.8 us -> 27.7 us
  transfers between devices with their start and end apart: 9 -> 11, of which waited for: 9 -> 10; matrix products, arithmetic and copies ran while one was open for 5% -> 6% of each run, Pallas kernels for 0% -> 0%
where the time goes in v1:
time: 772 us; the launch traced here: 762 us
  waiting for transfers between devices  516 us (67%)
  matrix products  97.3 us (13%)
  blocking collectives  43.7 us (6%)
  other arithmetic  35.4 us (5%)
  local copies, waits for them, and re-layouts  33.3 us (4%)
  starting transfers between devices  21.5 us (3%)
  between operations  15 us (2%)
    psum x1, waiting for transfers between devices, per_device(): lax.psum((grad_w_qkv, grad_w_attn_out, grad_w_in, grad_w_out), 'dp')  158 us
    reduce_scatter x1, waiting for transfers between devices, per_device(): lax.psum_scatter(jnp.einsum('cte,cde->td', grad_projected, w_qkv, preferr...  76.3 us
    reduce_scatter x1, waiting for transfers between devices, per_device(): lax.psum_scatter(jnp.einsum('tf,df->td', grad_hidden, w_in, preferred_ele...  75.3 us
    reduce_scatter x1, waiting for transfers between devices, per_device(): lax.psum_scatter(attn_part, 'mp', scatter_dimension=0, tiled=True)  75.1 us
    ppermute x3, waiting for transfers between devices, per_device(): lax.ppermute(ring[-1], 'mp', [(dev, (dev + 1) % 4) for dev in range(4)])  51 us
    all_gather x1, waiting for transfers between devices, per_device(): normed_all = lax.all_gather(normed, 'mp', axis=0, tiled=True)  44.8 us
    psum x1, blocking collectives, per_device(): lax.psum((gain_attn_part, gain_mlp_part), ('dp', 'mp'))  43.7 us
    all_gather x1, waiting for transfers between devices, per_device(): lax.all_gather(grad_resid.astype(jnp.bfloat16), 'mp', axis=0, tiled=True)  32.9 us
  transfers between devices with their start and end apart: 11, of which 10 were waited for; matrix products, arithmetic and copies ran while one was open for 6% of the time, Pallas kernels for 0%

profile of v1, /device:TPU:0, one launch (start us, length us, event | category | flops | bytes accessed | tf_op | source)
XLA Modules:
  0.0 762.3 jit_solution(13236756058929598485)
XLA Ops:
  14.7 44.8 %all-gather.4.cloned.1.call-done = bf16[1024,1024]{1,0:T(8,128)(2,1)} async-done(((bf16[256,1024]{1,0:T(8,128)(2,1)}), bf16[1024,1024]{1,0:T(8,128)(2,1)}) %all-gather.4.cloned.1.call-update) | async-done | bytes 2097168 | tf_op jit(solution)/shard_map/all_gather | solution.py:50
  83.5 75.1 %reduce-scatter.5.cloned.1.call-done = f32[256,1024]{1,0:T(8,128)} async-done(((f32[1024,1024]{1,0:T(8,128)}), f32[256,1024]{1,0:T(8,128)}) %reduce-scatter.5.cloned.1.call-update) | async-done | bytes 1048592 | tf_op jit(solution)/shard_map/reduce_scatter | solution.py:84
  162.8 18.2 %collective-permute-done = bf16[256,1024]{1,0:T(8,128)(2,1)S(1)} collective-permute-done((bf16[256,1024]{1,0:T(8,128)(2,1)}, bf16[256,1024]{1,0:T(8,128)(2,1)S(1)}, u32[]{:S(2)}, u32[]{:S(2)}) %collective-permute-start) | collective-permute-done | bytes 524320 | tf_op jit(solution)/shard_map/ppermute | solution.py:100
  181.8 6.2 collective-permute-start.1
  188.0 21.2 %collective-permute-done.1 = bf16[256,1024]{1,0:T(8,128)(2,1)} collective-permute-done((bf16[256,1024]{1,0:T(8,128)(2,1)S(1)}, bf16[256,1024]{1,0:T(8,128)(2,1)}, u32[]{:S(2)}, u32[]{:S(2)}) %collective-permute-start.1) | collective-permute-done | bytes 524320 | tf_op jit(solution)/shard_map/ppermute | solution.py:100
  209.2 12.8 %collective-permute-start.2 = (bf16[256,1024]{1,0:T(8,128)(2,1)}, bf16[256,1024]{1,0:T(8,128)(2,1)}, u32[]{:S(2)}, u32[]{:S(2)}) collective-permute-start(bf16[256,1024]{1,0:T(8,128)(2,1)} %collective-permute-done.1), channel_id=1, source_target_pairs={{0,1},{1,2},{2,3},{3,0},{4,5},{5,6},{6,7},{7,4},{8,9},{9,10},{10,1... | collective-permute-start | bytes 1572872 | tf_op jit(solution)/shard_map/ppermute | solution.py:100
  222.0 11.6 %collective-permute-done.2 = bf16[256,1024]{1,0:T(8,128)(2,1)} collective-permute-done((bf16[256,1024]{1,0:T(8,128)(2,1)}, bf16[256,1024]{1,0:T(8,128)(2,1)}, u32[]{:S(2)}, u32[]{:S(2)}) %collective-permute-start.2) | collective-permute-done | bytes 524320 | tf_op jit(solution)/shard_map/ppermute | solution.py:100
  250.5 8.0 %fusion.10 = bf16[1024,1024]{1,0:T(8,128)(2,1)S(1)} fusion(f32[1024,1024]{1,0:T(8,128)S(1)} %fusion.86, bf16[1024,1024]{1,0:T(8,128)(2,1)S(1)} %copy-done.34, bf16[2048,1024]{1,0:T(8,128)(2,1)} %constant_dynamic-update-slice_fusion, s32[]{:T(128)S(6)} %select_n.48), kind=kOutput, calls=%fused_computation.24 | convolution fusion | flops 2168455168 | bytes 10485764 | tf_op jit(solution)/shard_map/td,fd->tf/dot_general | solution.py:105
  259.8 4.4 fusion.87
  264.3 75.3 %reduce-scatter.9.cloned.1.call-done = f32[256,1024]{1,0:T(8,128)} async-done(((f32[1024,1024]{1,0:T(8,128)}), f32[256,1024]{1,0:T(8,128)}) %reduce-scatter.9.cloned.1.call-update) | async-done | bytes 1048592 | tf_op jit(solution)/shard_map/reduce_scatter | solution.py:110
  343.7 6.8 fusion.90
  350.5 6.6 fusion.26
  357.1 32.9 %all-gather.8.cloned.1.call-done = bf16[1024,1024]{1,0:T(8,128)(2,1)} async-done(((bf16[256,1024]{1,0:T(8,128)(2,1)}), bf16[1024,1024]{1,0:T(8,128)(2,1)}) %all-gather.8.cloned.1.call-update) | async-done | bytes 2097168 | tf_op jit(solution)/shard_map/all_gather | solution.py:118
  392.6 5.2 fusion.11
  397.8 5.8 multiply_reduce_fusion
  403.6 5.8 multiply_reduce_fusion.1
  409.4 10.5 %multiply_convert_fusion = (bf16[4,512,1024]{2,1,0:T(8,128)(2,1)}, bf16[4,512,1024]{2,1,0:T(8,128)(2,1)S(1)}) fusion(f32[4,512,1024]{2,1,0:T(8,128)} %get-tuple-element.55, f32[4,512]{1,0:T(4,128)S(1)} %get-tuple-element.54, f32[4,512]{1,0:T(4,128)S(1)} %log_add_fusion, f32[4,512,1024]{2,1,0:T(8,128)S(1)} %bitcast.81, pred[512,1024]{1,0:T(8,128)(4,1)S(1)} %copy-done.12, ...), kind=kLoop, calls=%fused_computation | loop fusion | flops 29360128 | bytes 43024384 | tf_op jit(solution)/shard_map/convert_element_type | solution.py:149
  428.2 4.4 fusion.54
  440.0 5.3 fusion.23
  446.3 5.2 convolution_bitcast_fusion
  453.2 6.2 convolution_convert_fusion
  459.5 158.1 %all-reduce.4.cloned.1.call-done = (f32[3,1024,256]{1,2,0:T(8,128)}, f32[256,1024]{1,0:T(8,128)}, f32[1024,1024]{1,0:T(8,128)}, f32[1024,1024]{1,0:T(8,128)}) async-done(((f32[3,1024,256]{1,2,0:T(8,128)}, f32[256,1024]{1,0:T(8,128)}, f32[1024,1024]{1,0:T(8,128)}, f32[1024,1024]{1,0:T(8,128)}), (f32[3,1024,256]{1,2,0:T(8,128)}, f32[256,1024]{1,0:T(8,128)}, f32[1024,1024]{1,0:T(8,128)}, ...) | async-done | bytes 12582928 | tf_op jit(solution)/shard_map/psum | solution.py:180
  621.1 76.3 %reduce-scatter.11.cloned.1.call-done = f32[256,1024]{1,0:T(8,128)} async-done(((f32[1024,1024]{1,0:T(8,128)}), f32[256,1024]{1,0:T(8,128)}) %reduce-scatter.11.cloned.1.call-update) | async-done | bytes 1048592 | tf_op jit(solution)/shard_map/reduce_scatter | solution.py:171
  699.0 43.7 %all-reduce = (f32[1024]{0:T(1024)}, f32[1024]{0:T(1024)}) all-reduce(f32[1024]{0:T(1024)S(1)} %get-tuple-element.26, f32[1024]{0:T(1024)S(1)} %get-tuple-element.24), channel_id=1, replica_groups=mesh['dp'=8,'mp'=4] {'dp','mp'}, use_global_device_ids=true, to_apply=%region_21.22 | all-reduce | flops 2048 | bytes 16384 | tf_op jit(solution)/shard_map/psum | solution.py:179
  (166 shorter events, 96.8 us)
Async XLA Ops:
  7.2 239.3 %copy-start = (bf16[1024,1024]{1,0:T(8,128)(2,1)S(1)}, bf16[1024,1024]{1,0:T(8,128)(2,1)}, u32[]{:S(2)}) copy-start(bf16[1024,1024]{1,0:T(8,128)(2,1)} %param.13) | copy-start | bytes 6291460
  7.2 52.3 %all-gather.4.cloned.1.call-start = ((), (), s32[]{:S(2)}) async-start(), calls=%async_computation.4 | async-start | bytes 2621440 | tf_op jit(solution)/shard_map/all_gather | solution.py:50
  10.7 148.0 %reduce-scatter.5.cloned.1.call-start = ((), (), s32[]{:S(2)}) async-start(), calls=%async_computation.5 | async-start | bytes 5242880 | tf_op jit(solution)/shard_map/reduce_scatter | solution.py:84
  14.7 61.8 %copy-start.9 = (pred[512,1024]{1,0:T(8,128)(4,1)}, pred[512,1024]{1,0:T(8,128)(4,1)S(1)}, u32[]{:S(2)}) copy-start(pred[512,1024]{1,0:T(8,128)(4,1)S(1)} %get-tuple-element.44) | copy-start | bytes 1572868
  63.5 12.9 %copy-start.30 = (bf16[1,1024,256]{1,2,0:T(8,128)(2,1)}, bf16[1,1024,256]{1,2,0:T(8,128)(2,1)S(1)}, u32[]{:S(2)}) copy-start(bf16[1,1024,256]{1,2,0:T(8,128)(2,1)S(1)} %get-tuple-element.39) | copy-start | bytes 1572868
  83.0 77.2 %copy-start.32 = (f32[1024]{0:T(1024)S(1)}, f32[1024]{0:T(1024)}, u32[]{:S(2)}) copy-start(f32[1024]{0:T(1024)} %param.16) | copy-start | bytes 12292
  83.0 163.5 %all-gather.6.cloned.1.call-start = ((), (), s32[]{:S(2)}) async-start(), calls=%async_computation.6 | async-start | bytes 2621440 | tf_op jit(solution)/shard_map/all_gather | solution.py:87
  161.2 178.4 %reduce-scatter.9.cloned.1.call-start = ((), (), s32[]{:S(2)}) async-start(), calls=%async_computation.8 | async-start | bytes 5242880 | tf_op jit(solution)/shard_map/reduce_scatter | solution.py:110
  161.2 19.7 %collective-permute-start = (bf16[256,1024]{1,0:T(8,128)(2,1)}, bf16[256,1024]{1,0:T(8,128)(2,1)S(1)}, u32[]{:S(2)}, u32[]{:S(2)}) collective-permute-start(bf16[256,1024]{1,0:T(8,128)(2,1)} %param.17), channel_id=1, source_target_pairs={{0,1},{1,2},{2,3},{3,0},{4,5},{5,6},{6,7},{7,4},{8,9},{9,10},{10,1... | collective-permute-start | bytes 1572872 | tf_op jit(solution)/shard_map/ppermute | solution.py:100
  181.8 27.4 %collective-permute-start.1 = (bf16[256,1024]{1,0:T(8,128)(2,1)S(1)}, bf16[256,1024]{1,0:T(8,128)(2,1)}, u32[]{:S(2)}, u32[]{:S(2)}) collective-permute-start(bf16[256,1024]{1,0:T(8,128)(2,1)S(1)} %collective-permute-done), channel_id=1, source_target_pairs={{0,1},{1,2},{2,3},{3,0},{4,5},{5,6},{6,7},{7,4},{8,9},{9,10},{10,1... | collective-permute-start | bytes 1572872 | tf_op jit(solution)/shard_map/ppermute | solution.py:100
  209.2 24.4 %collective-permute-start.2 = (bf16[256,1024]{1,0:T(8,128)(2,1)}, bf16[256,1024]{1,0:T(8,128)(2,1)}, u32[]{:S(2)}, u32[]{:S(2)}) collective-permute-start(bf16[256,1024]{1,0:T(8,128)(2,1)} %collective-permute-done.1), channel_id=1, source_target_pairs={{0,1},{1,2},{2,3},{3,0},{4,5},{5,6},{6,7},{7,4},{8,9},{9,10},{10,1... | collective-permute-start | bytes 1572872 | tf_op jit(solution)/shard_map/ppermute | solution.py:100
  222.0 22.8 %copy-start.23 = (bf16[256,1024]{1,0:T(8,128)(2,1)S(1)}, bf16[256,1024]{1,0:T(8,128)(2,1)}, u32[]{:S(2)}) copy-start(bf16[256,1024]{1,0:T(8,128)(2,1)} %copy-done.22) | copy-start | bytes 1572868
  222.0 23.6 %copy-start.13 = (bf16[256,1024]{1,0:T(8,128)(2,1)S(1)}, bf16[256,1024]{1,0:T(8,128)(2,1)}, u32[]{:S(2)}) copy-start(bf16[256,1024]{1,0:T(8,128)(2,1)} %param.17) | copy-start | bytes 1572868
  264.2 76.9 %copy-start.14 = (bf16[256,1024]{1,0:T(8,128)(2,1)S(1)}, bf16[256,1024]{1,0:T(8,128)(2,1)}, u32[]{:S(2)}) copy-start(bf16[256,1024]{1,0:T(8,128)(2,1)} %param.17) | copy-start | bytes 1572868
  264.3 125.8 %all-gather.8.cloned.1.call-start = ((), (), s32[]{:S(2)}) async-start(), calls=%async_computation.9 | async-start | bytes 2621440 | tf_op jit(solution)/shard_map/all_gather | solution.py:118
  343.5 274.1 %all-reduce.4.cloned.1.call-start = ((), (), s32[]{:S(2)}) async-start(), calls=%async_computation.11 | async-start | bytes 25165824 | tf_op jit(solution)/shard_map/psum | solution.py:180
  350.5 39.6 %copy-start.26 = (bf16[256,1024]{1,0:T(8,128)(2,1)S(1)}, bf16[256,1024]{1,0:T(8,128)(2,1)}, u32[]{:S(2)}) copy-start(bf16[256,1024]{1,0:T(8,128)(2,1)} %param.12) | copy-start | bytes 1572868
  357.1 35.5 %copy-start.12 = (pred[512,1024]{1,0:T(8,128)(4,1)S(1)}, pred[512,1024]{1,0:T(8,128)(4,1)}, u32[]{:S(2)}) copy-start(pred[512,1024]{1,0:T(8,128)(4,1)} %get-tuple-element.45) | copy-start | bytes 1572868
  445.3 252.1 %reduce-scatter.11.cloned.1.call-start = ((), (), s32[]{:S(2)}) async-start(), calls=%async_computation.10 | async-start | bytes 5242880 | tf_op jit(solution)/shard_map/reduce_scatter | solution.py:171
  451.6 293.6 %reduce-scatter.7.cloned.1.call-start = ((), (), s32[]{:S(2)}) async-start(), calls=%async_computation.7 | async-start | bytes 2621440 | tf_op jit(solution)/shard_map/reduce_scatter | solution.py:90
  459.4 238.1 %copy-start.7 = (bf16[256,1024]{1,0:T(8,128)(2,1)S(1)}, bf16[256,1024]{1,0:T(8,128)(2,1)}, u32[]{:S(2)}) copy-start(bf16[256,1024]{1,0:T(8,128)(2,1)} %param.9) | copy-start | bytes 1572868
  459.4 238.1 %copy-start.33 = (f32[1024]{0:T(1024)S(1)}, f32[1024]{0:T(1024)}, u32[]{:S(2)}) copy-start(f32[1024]{0:T(1024)} %param.15) | copy-start | bytes 12292
  459.4 285.7 %copy-start.8 = (f32[256,1024]{1,0:T(8,128)S(1)}, f32[256,1024]{1,0:T(8,128)}, u32[]{:S(2)}) copy-start(f32[256,1024]{1,0:T(8,128)} %reduce-scatter.9.cloned.1.call-done) | copy-start | bytes 3145732
  459.4 285.7 %copy-start.15 = (bf16[256,1024]{1,0:T(8,128)(2,1)S(1)}, bf16[256,1024]{1,0:T(8,128)(2,1)}, u32[]{:S(2)}) copy-start(bf16[256,1024]{1,0:T(8,128)(2,1)} %param.17) | copy-start | bytes 1572868
  (30 other events, 147.5 us)
Sparse Core Ops, SparseCore 0:
  10.8 48.6 all-gather.3
  83.1 75.4 reduce-scatter.4
  161.3 62.1 all-gather.5
  264.4 75.1 reduce-scatter.8
  343.6 46.4 all-gather.7
  445.4 172.0 all-reduce.3
  620.6 76.8 reduce-scatter.10
  699.8 45.3 reduce-scatter.6
